TPU v7x, 128 devices: a whole 4x4x4 slice. The times are simulated.
128 devices in a mesh: expert: 8 (over x, core), panel: 16 (over y, z).
Axes of the slice: x: 4, y: 4, z: 4, core: 2. Of those that a mesh axis runs over, the one named last changes fastest.
Arguments:
- activations: bfloat16 [2, 128, 96, 6144], P(None, ('expert', 'panel')), may hold values from -6 to 6
- gradients: bfloat16 [2, 128, 96, 16384], P(None, ('expert', 'panel')), may hold values from -6 to 6
- expert_ids: int32 [2, 128, 96, 1], P(None, ('expert', 'panel')), may hold values from 0 to 7; in each aligned block of 96 rows (0 to 95, 96 to 191, ..., all dimensions but the last counted through in order) at most 18 rows name the same one
- sequence_ids: int32 [2, 128, 96], P(None, ('expert', 'panel')), may hold values from 0 to 3, never falling along the last dimension, each value on 1 to 48 neighbouring positions
- input_basis: bfloat16 [8, 6144, 384], P('expert', 'panel'), may hold values from -0.078125 to 0.078125
- output_basis: bfloat16 [8, 16384, 256], P('expert', 'panel'), may hold values from -0.046875 to 0.046875
Outputs:
- corrected_eigenvalues: float32 [8, 384, 256], P('expert', 'panel')
Inputs may be any that keep to these rules, and one draw needn't show every extreme that they name: `expert_ids`: among the 96 rows of one device block of one microbatch, no expert is named by more than 18 rows; some block names some expert exactly 18 times; every expert is named somewhere. `sequence_ids`: within a device block of one microbatch the numbers never fall, and each of the 4 sequences holds 1 to 48 rows.
All inputs are finite; a program needn't handle non-finite values.
Results may differ from a plain program's by a relative error of at most 0.00083.
Values may be sent and summed in bfloat16 or wider, within the bound.
A program may use at most 128 MiB of HBM per device.

v0:
```python
import jax
import jax.numpy as jnp
from jax import lax
from jax.sharding import PartitionSpec as P

SEQ_DEV = 4


def cut_along(value, dim, size):
    before, after = (value.shape[:dim], value.shape[dim + 1 :])
    return jnp.moveaxis(value.reshape(*before, size, -1, *after), dim, 0)


def sent_and_summed(value, axis, dim):
    pieces = cut_along(value, dim, lax.axis_size(axis))
    arrived = lax.all_to_all(pieces, axis, split_axis=0, concat_axis=0, tiled=True)
    return arrived.sum(axis=0)


def pack_rows(inputs, grads, ids, seqs, experts, capacity):
    tokens = ids.shape[0]
    onehot = (ids[:, None] == jnp.arange(experts, dtype=jnp.int32)[None, :]).astype(jnp.int32)
    before = jnp.cumsum(onehot, axis=0) - onehot
    offset = jnp.sum(before * onehot, axis=1)
    target = ids * capacity + offset
    placed = target[:, None] == jnp.arange(experts * capacity, dtype=jnp.int32)[None, :]
    source = jnp.sum(jnp.where(placed, jnp.arange(tokens, dtype=jnp.int32)[:, None], 0), axis=0)
    filled = jnp.any(placed, axis=0)
    input_rows = jnp.where(filled[:, None], inputs[source], jnp.zeros((), inputs.dtype))
    grad_rows = jnp.where(filled[:, None], grads[source], jnp.zeros((), grads.dtype))
    labels = jnp.where(filled, seqs[source] + 1, 0)
    width_in = inputs.shape[1]
    width_out = grads.shape[1]
    return (
        input_rows.reshape(experts, capacity, width_in),
        grad_rows.reshape(experts, capacity, width_out),
        labels.reshape(experts, capacity),
    )


def receive_rows(activations, gradients, expert_ids, sequence_ids, batch_index, experts, capacity):
    packed = pack_rows(
        activations[batch_index, 0],
        gradients[batch_index, 0],
        expert_ids[batch_index, 0, :, 0],
        sequence_ids[batch_index, 0],
        experts,
        capacity,
    )
    return (
        lax.all_to_all(packed[0], "expert", split_axis=0, concat_axis=0, tiled=True),
        lax.all_to_all(packed[1], "expert", split_axis=0, concat_axis=0, tiled=True),
        lax.all_to_all(packed[2], "expert", split_axis=0, concat_axis=0, tiled=True),
    )


def rotate_rows(input_rows, grad_rows, labels, input_basis, output_basis):
    capacity = input_rows.shape[1]
    count = input_rows.shape[0] * capacity
    flat_in = input_rows.reshape(count, input_rows.shape[2])
    flat_grad = grad_rows.reshape(count, grad_rows.shape[2])
    width_a = input_basis.shape[2]
    width_g = output_basis.shape[2]
    columns = flat_in
    rotated_in = jnp.dot(
        columns,
        lax.all_gather(input_basis[0], "panel", axis=0, tiled=True),
        preferred_element_type=jnp.float32,
    )
    columns = flat_grad
    rotated_out = jnp.dot(
        columns,
        lax.all_gather(output_basis[0], "panel", axis=0, tiled=True),
        preferred_element_type=jnp.float32,
    )
    own_labels = labels.reshape(count)
    return (
        rotated_in.astype(jnp.bfloat16).reshape(-1, capacity, width_a),
        rotated_out.astype(jnp.bfloat16).reshape(-1, capacity, width_g),
        own_labels.reshape(-1, capacity),
    )


def contract(rotated_inputs, rotated_grads, labels):
    member = (
        labels[:, :, None] == jnp.arange(1, SEQ_DEV + 1, dtype=jnp.int32)[None, None, :]
    ).astype(jnp.bfloat16)
    masked = jnp.transpose(member, (0, 2, 1))[:, :, :, None] * rotated_inputs[:, None, :, :]
    per_seq = jnp.einsum(
        "sjca,scg->sjag", masked, rotated_grads, preferred_element_type=jnp.float32
    )
    return jnp.sum(per_seq * per_seq, axis=(0, 1))


def per_device(activations, gradients, expert_ids, sequence_ids, input_basis, output_basis):
    experts = lax.axis_size("expert")
    panels = lax.axis_size("panel")
    batches = activations.shape[0]
    capacity = activations.shape[2] * 3 // (2 * experts)
    received = [
        receive_rows(
            activations, gradients, expert_ids, sequence_ids, batch_index, experts, capacity
        )
        for batch_index in range(batches)
    ]
    input_rows = jnp.concatenate([item[0] for item in received], axis=0)
    grad_rows = jnp.concatenate([item[1] for item in received], axis=0)
    labels = jnp.concatenate([item[2] for item in received], axis=0)
    rotated_in, rotated_out, own_labels = rotate_rows(
        input_rows, grad_rows, labels, input_basis, output_basis
    )
    running = contract(rotated_in, rotated_out, own_labels)
    summed = sent_and_summed(running[None], "panel", 1)
    return summed / (batches * experts * panels * SEQ_DEV)


def solution(mesh):
    placed = (
        P(None, ("expert", "panel"), None, None),
        P(None, ("expert", "panel"), None, None),
        P(None, ("expert", "panel"), None, None),
        P(None, ("expert", "panel"), None),
        P("expert", "panel", None),
        P("expert", "panel", None),
    )
    return jax.shard_map(
        per_device,
        mesh=mesh,
        in_specs=placed,
        out_specs=P("expert", "panel", None),
        check_vma=False,
    )
```

profile of v0, /device:TPU:0, one launch (start us, length us, event | category | flops | bytes accessed | tf_op | source)
XLA Modules:
  0.0 329.8 jit_solution(9472606236988926837)
XLA Ops:
  12.4 4.4 %all-to-all-start = ((s32[8,1,18]{2,1,0:T(1,128)}), s32[8,1,18]{2,1,0:T(1,128)S(1)}, u32[]{:S(2)}, u32[]{:S(2)}) async-start(s32[8,1,18]{2,1,0:T(1,128)} %select_n.81), calls=%async_computation | async-start | bytes 8192 | tf_op jit(solution)/shard_map/all_to_all | solution.py:53
  27.7 4.8 %all-to-all-start.1 = ((s32[8,1,18]{2,1,0:T(1,128)}), s32[8,1,18]{2,1,0:T(1,128)S(1)}, u32[]{:S(2)}, u32[]{:S(2)}) async-start(s32[8,1,18]{2,1,0:T(1,128)} %select_n.85), calls=%async_computation.1 | async-start | bytes 8192 | tf_op jit(solution)/shard_map/all_to_all | solution.py:53
  37.7 4.6 %all-to-all-start.2 = ((bf16[8,18,6144]{2,1,0:T(8,128)(2,1)}), bf16[8,18,6144]{2,1,0:T(8,128)(2,1)}, u32[]{:S(2)}, u32[]{:S(2)}) async-start(bf16[8,18,6144]{2,1,0:T(8,128)(2,1)} %broadcast_select_fusion.3), calls=%async_computation.2 | async-start | bytes 4718592 | tf_op jit(solution)/shard_map/all_to_all | solution.py:51
  42.3 5.4 %slice_bitcast_fusion.1 = (bf16[96,16384]{1,0:T(8,128)(2,1)}, bf16[96,16384]{1,0:T(8,128)(2,1)S(1)}) fusion(bf16[2,1,96,16384]{3,2,1,0:T(8,128)(2,1)} %param.7), kind=kLoop, calls=%fused_computation.16 | loop fusion | bytes 12582912 | tf_op jit(solution)/shard_map/squeeze | solution.py:44
  47.8 12.1 %gather_fusion.4 = bf16[144,16384]{1,0:T(8,128)(2,1)} fusion(bf16[96,16384]{1,0:T(8,128)(2,1)} %get-tuple-element.5, s32[1024]{0:T(1024)S(1)} %pad_clamp_fusion.1), kind=kCustom, calls=%fused_computation.4 | custom fusion | bytes 9437760 | tf_op jit(solution)/shard_map/gather | solution.py:30
  59.9 5.2 %gather.33 = bf16[8,18,16384]{2,1,0:T(8,128)(2,1)} reshape(bf16[144,16384]{1,0:T(8,128)(2,1)} %gather_fusion.4) | data formatting | bytes 9437184 | tf_op jit(solution)/shard_map/gather | solution.py:30
  65.0 5.9 %gather_fusion.3 = bf16[144,6144]{1,0:T(8,128)(2,1)} fusion(bf16[96,6144]{1,0:T(8,128)(2,1)} %get-tuple-element.8, s32[1024]{0:T(1024)S(1)} %pad_clamp_fusion), kind=kCustom, calls=%fused_computation.3 | custom fusion | bytes 3539520 | tf_op jit(solution)/shard_map/gather | solution.py:29
  77.3 4.5 %all-to-all-start.3 = ((bf16[8,18,6144]{2,1,0:T(8,128)(2,1)}), bf16[8,18,6144]{2,1,0:T(8,128)(2,1)}, u32[]{:S(2)}, u32[]{:S(2)}) async-start(bf16[8,18,6144]{2,1,0:T(8,128)(2,1)} %broadcast_select_fusion.2), calls=%async_computation.3 | async-start | bytes 4718592 | tf_op jit(solution)/shard_map/all_to_all | solution.py:51
  81.8 5.9 %broadcast_select_fusion.1 = bf16[8,18,16384]{2,1,0:T(8,128)(2,1)} fusion(bf16[8,18,16384]{2,1,0:T(8,128)(2,1)} %gather.33, pred[8,18]{1,0:T(8,128)(4,1)S(1)} %broadcast_in_dim.84), kind=kLoop, calls=%fused_computation.11 | loop fusion | flops 2359296 | bytes 9437328 | tf_op jit(solution)/shard_map/jit(_where)/select_n | solution.py:30
  87.7 24.2 %all-to-all-done.3 = bf16[8,18,6144]{2,1,0:T(8,128)(2,1)} async-done(((bf16[8,18,6144]{2,1,0:T(8,128)(2,1)}), bf16[8,18,6144]{2,1,0:T(8,128)(2,1)}, u32[]{:S(2)}, u32[]{:S(2)}) %all-to-all-start.3) | async-done | bytes 1769504 | tf_op jit(solution)/shard_map/all_to_all | solution.py:51
  111.9 4.8 %all-to-all-start.4 = ((bf16[8,18,16384]{2,1,0:T(8,128)(2,1)}), bf16[8,18,16384]{2,1,0:T(8,128)(2,1)}, u32[]{:S(2)}, u32[]{:S(2)}) async-start(bf16[8,18,16384]{2,1,0:T(8,128)(2,1)} %broadcast_select_fusion.1), calls=%async_computation.4 | async-start | bytes 12582912 | tf_op jit(solution)/shard_map/all_to_all | solution.py:52
  116.7 5.6 %gather_fusion.5 = bf16[144,16384]{1,0:T(8,128)(2,1)} fusion(bf16[96,16384]{1,0:T(8,128)(2,1)S(1)} %get-tuple-element.6, s32[1024]{0:T(1024)S(1)} %pad_clamp_fusion), kind=kCustom, calls=%fused_computation.5 | custom fusion | bytes 9437760 | tf_op jit(solution)/shard_map/gather | solution.py:30
  122.3 5.3 %gather.35 = bf16[8,18,16384]{2,1,0:T(8,128)(2,1)} reshape(bf16[144,16384]{1,0:T(8,128)(2,1)} %gather_fusion.5) | data formatting | bytes 9437184 | tf_op jit(solution)/shard_map/gather | solution.py:30
  127.6 6.0 %broadcast_select_fusion = bf16[8,18,16384]{2,1,0:T(8,128)(2,1)} fusion(bf16[8,18,16384]{2,1,0:T(8,128)(2,1)} %gather.35, pred[8,18]{1,0:T(8,128)(4,1)S(1)} %broadcast_in_dim.87), kind=kLoop, calls=%fused_computation.10 | loop fusion | flops 2359296 | bytes 9437328 | tf_op jit(solution)/shard_map/jit(_where)/select_n | solution.py:30
  133.6 55.2 %all-to-all-done.4 = bf16[8,18,16384]{2,1,0:T(8,128)(2,1)} async-done(((bf16[8,18,16384]{2,1,0:T(8,128)(2,1)}), bf16[8,18,16384]{2,1,0:T(8,128)(2,1)}, u32[]{:S(2)}, u32[]{:S(2)}) %all-to-all-start.4) | async-done | bytes 4718624 | tf_op jit(solution)/shard_map/all_to_all | solution.py:52
  188.8 5.0 %all-to-all-start.5 = ((bf16[8,18,16384]{2,1,0:T(8,128)(2,1)}), bf16[8,18,16384]{2,1,0:T(8,128)(2,1)}, u32[]{:S(2)}, u32[]{:S(2)}) async-start(bf16[8,18,16384]{2,1,0:T(8,128)(2,1)} %broadcast_select_fusion), calls=%async_computation.5 | async-start | bytes 12582912 | tf_op jit(solution)/shard_map/all_to_all | solution.py:52
  193.9 5.0 %pad_maximum_fusion.1 = bf16[16,18,6144]{2,1,0:T(8,128)(2,1)} fusion(bf16[8,18,6144]{2,1,0:T(8,128)(2,1)} %all-to-all-done.3, bf16[8,18,6144]{2,1,0:T(8,128)(2,1)} %all-to-all-done.2), kind=kLoop, calls=%fused_computation.12 | loop fusion | flops 1769472 | bytes 7077888 | tf_op jit(solution)/shard_map/concatenate | solution.py:106
  202.6 63.1 %all-to-all-done.5 = bf16[8,18,16384]{2,1,0:T(8,128)(2,1)} async-done(((bf16[8,18,16384]{2,1,0:T(8,128)(2,1)}), bf16[8,18,16384]{2,1,0:T(8,128)(2,1)}, u32[]{:S(2)}, u32[]{:S(2)}) %all-to-all-start.5) | async-done | bytes 4718624 | tf_op jit(solution)/shard_map/all_to_all | solution.py:52
  265.7 11.1 %pad_maximum_fusion = bf16[16,18,16384]{2,1,0:T(8,128)(2,1)} fusion(bf16[8,18,16384]{2,1,0:T(8,128)(2,1)} %all-to-all-done.5, bf16[8,18,16384]{2,1,0:T(8,128)(2,1)} %all-to-all-done.4), kind=kLoop, calls=%fused_computation.7 | loop fusion | flops 4718592 | bytes 18874368 | tf_op jit(solution)/shard_map/concatenate | solution.py:107
  276.8 9.5 %reshape.159 = bf16[288,16384]{1,0:T(8,128)(2,1)} reshape(bf16[16,18,16384]{2,1,0:T(8,128)(2,1)} %pad_maximum_fusion) | data formatting | bytes 18874368 | tf_op jit(solution)/shard_map/reshape | solution.py:61
  286.3 5.0 %fusion.4 = bf16[288,384]{1,0:T(8,128)(2,1)} fusion(bf16[288,6144]{1,0:T(8,128)(2,1)S(1)} %reshape.158, bf16[1,6144,384]{2,1,0:T(8,128)(2,1)} %all-gather.5.cloned.1.call-done), kind=kOutput, calls=%fused_computation.19 | convolution fusion | flops 1359065088 | bytes 8478720 | tf_op jit(solution)/shard_map/dot_general | solution.py:65
  292.4 8.7 %fusion.8 = bf16[288,256]{1,0:T(8,128)(2,1)S(1)} fusion(bf16[288,16384]{1,0:T(8,128)(2,1)} %reshape.159, bf16[1,16384,256]{2,1,0:T(8,128)(2,1)} %all-gather.7.cloned.1.call-done), kind=kOutput, calls=%fused_computation.23 | convolution fusion | flops 2415992832 | bytes 17973248 | tf_op jit(solution)/shard_map/dot_general | solution.py:71
  301.1 4.3 %multiply_reduce_fusion = f32[384,256]{1,0:T(8,128)S(1)} fusion(bf16[16,18,384]{2,1,0:T(8,128)(2,1)S(1)} %mul.43, bf16[16,4,18]{2,1,0:T(4,128)(2,1)S(1)} %compare_convert_fusion, bf16[16,18,256,1]{2,1,0,3:T(8,128)(2,1)S(1)} %reshape.211), kind=kOutput, calls=%fused_computation.6 | convolution fusion | flops 239419392 | bytes 764160 | tf_op jit(solution)/shard_map/sjca,scg->sjag/dot_general | solution.py:89
  305.4 16.9 %all_to_all.43 = f32[16,1,24,256]{3,2,1,0:T(8,128)S(1)} all-to-all(f32[16,1,24,256]{3,2,1,0:T(8,128)S(1)} %bitcast.44), channel_id=1, replica_groups=mesh['expert'=8,'panel'=16] {'panel'}, dimensions={0} | all-to-all | bytes 786432 | tf_op jit(solution)/shard_map/all_to_all | solution.py:16
  (47 shorter events, 33.6 us)
Async XLA Ops:
  6.5 279.8 %all-gather.5.cloned.1.call-start = ((), (), s32[]{:S(2)}) async-start(), calls=%async_computation.7 | async-start | bytes 5013504 | tf_op jit(solution)/shard_map/all_gather | solution.py:67
  12.4 15.3 %all-to-all-start = ((s32[8,1,18]{2,1,0:T(1,128)}), s32[8,1,18]{2,1,0:T(1,128)S(1)}, u32[]{:S(2)}, u32[]{:S(2)}) async-start(s32[8,1,18]{2,1,0:T(1,128)} %select_n.81), calls=%async_computation | async-start | bytes 8192 | tf_op jit(solution)/shard_map/all_to_all | solution.py:53
  16.8 275.5 %all-gather.7.cloned.1.call-start = ((), (), s32[]{:S(2)}) async-start(), calls=%async_computation.8 | async-start | bytes 8912896 | tf_op jit(solution)/shard_map/all_gather | solution.py:73
  27.7 10.0 %all-to-all-start.1 = ((s32[8,1,18]{2,1,0:T(1,128)}), s32[8,1,18]{2,1,0:T(1,128)S(1)}, u32[]{:S(2)}, u32[]{:S(2)}) async-start(s32[8,1,18]{2,1,0:T(1,128)} %select_n.85), calls=%async_computation.1 | async-start | bytes 8192 | tf_op jit(solution)/shard_map/all_to_all | solution.py:53
  37.7 39.6 %all-to-all-start.2 = ((bf16[8,18,6144]{2,1,0:T(8,128)(2,1)}), bf16[8,18,6144]{2,1,0:T(8,128)(2,1)}, u32[]{:S(2)}, u32[]{:S(2)}) async-start(bf16[8,18,6144]{2,1,0:T(8,128)(2,1)} %broadcast_select_fusion.3), calls=%async_computation.2 | async-start | bytes 4718592 | tf_op jit(solution)/shard_map/all_to_all | solution.py:51
  77.3 34.6 %all-to-all-start.3 = ((bf16[8,18,6144]{2,1,0:T(8,128)(2,1)}), bf16[8,18,6144]{2,1,0:T(8,128)(2,1)}, u32[]{:S(2)}, u32[]{:S(2)}) async-start(bf16[8,18,6144]{2,1,0:T(8,128)(2,1)} %broadcast_select_fusion.2), calls=%async_computation.3 | async-start | bytes 4718592 | tf_op jit(solution)/shard_map/all_to_all | solution.py:51
  111.9 76.9 %all-to-all-start.4 = ((bf16[8,18,16384]{2,1,0:T(8,128)(2,1)}), bf16[8,18,16384]{2,1,0:T(8,128)(2,1)}, u32[]{:S(2)}, u32[]{:S(2)}) async-start(bf16[8,18,16384]{2,1,0:T(8,128)(2,1)} %broadcast_select_fusion.1), calls=%async_computation.4 | async-start | bytes 12582912 | tf_op jit(solution)/shard_map/all_to_all | solution.py:52
  188.8 76.9 %all-to-all-start.5 = ((bf16[8,18,16384]{2,1,0:T(8,128)(2,1)}), bf16[8,18,16384]{2,1,0:T(8,128)(2,1)}, u32[]{:S(2)}, u32[]{:S(2)}) async-start(bf16[8,18,16384]{2,1,0:T(8,128)(2,1)} %broadcast_select_fusion), calls=%async_computation.5 | async-start | bytes 12582912 | tf_op jit(solution)/shard_map/all_to_all | solution.py:52
Sparse Core Ops, SparseCore 0:
  9.5 56.4 all-gather.4
  68.1 70.5 all-gather.6
where the time goes:
time: 331 us; the launch traced here: 330 us
  waiting for transfers between devices  147 us (44%)
  local copies, waits for them, and re-layouts  70.1 us (21%)
  other arithmetic  35.6 us (11%)
  starting transfers between devices  28.1 us (8%)
  matrix products  17.9 us (5%)
  blocking collectives  16.9 us (5%)
  between operations  13.6 us (4%)
    all_to_all x2, waiting for transfers between devices, receive_rows(): lax.all_to_all(packed[1], 'expert', split_axis=0, concat_axis=0, tiled=True)  118 us
    gather x4, local copies, waits for them, and re-layouts, pack_rows(): grads[source]  28.2 us
    all_to_all x2, waiting for transfers between devices, receive_rows(): lax.all_to_all(packed[0], 'expert', split_axis=0, concat_axis=0, tiled=True)  24.2 us
    all_to_all x1, blocking collectives, sent_and_summed(): lax.all_to_all(pieces, axis, split_axis=0, concat_axis=0, tiled=True)  16.9 us
    gather x4, local copies, waits for them, and re-layouts, pack_rows(): inputs[source]  13.5 us
    select_n x2, other arithmetic, pack_rows(): jnp.where(filled[:, None], grads[source], jnp.zeros((), grads.dtype))  11.9 us
    concatenate x1, other arithmetic, per_device(): grad_rows = jnp.concatenate([item[1] for item in received], axis=0)  11.1 us
    all_to_all x2, starting transfers between devices, receive_rows(): lax.all_to_all(packed[1], 'expert', split_axis=0, concat_axis=0, tiled=True)  9.82 us
  transfers between devices with their start and end apart: 8, of which 4 were waited for; matrix products, arithmetic and copies ran while one was open for 33% of the time, Pallas kernels for 0%

commit v1 on v0

v1 whole, which is shorter than its diff:
```python
import functools

import jax
import jax.numpy as jnp
from jax import lax
from jax.experimental import pallas as pl
from jax.experimental.pallas import tpu as pltpu
from jax.sharding import PartitionSpec as P

MESH = pl.DeviceIdType.MESH
SEQS = 4
N = 4
CAP = 18
PAIR = 48
TAG = 1024
BF16 = jnp.bfloat16
F32 = jnp.float32


def kernel(sizes, *refs):
    (codes, act, grad, ibs, gbs, out) = refs[:6]
    (cz, cy, gx, ix, gb, ib, pg, pi, go, io, rg, ri, rs, ra, acc, fr) = refs[6:22]
    (s_send, s_cz, s_cy, s_gx, s_ix, s_loc, s_a, s_p, s_rg, s_ri, s_ra, s_fr) = refs[22:]
    toks, wa, wg, ka, kg, rows = sizes
    ga, gg = wa // N, wg // N
    pa, pgc = ga // N, gg // N
    e = lax.axis_index("expert")
    p = lax.axis_index("panel")
    x, c = e // 2, e % 2
    y, z = p // N, p % N
    other = 1 - c

    def dev(xx, yy, zz, cc):
        return (2 * xx + cc, N * yy + zz)

    def up(i, d):
        return (i + d) % N

    sends = []

    def send(src, dst, sem, device, when=None):
        i = len(sends)
        copy = pltpu.make_async_remote_copy(
            src_ref=src,
            dst_ref=dst,
            send_sem=s_send.at[i],
            recv_sem=sem,
            device_id=device,
            device_id_type=MESH,
        )
        sends.append((copy, when))
        if when is None:
            copy.start()
        else:
            pl.when(when)(lambda: copy.start())

    def arrived(ref, sem):
        pltpu.make_async_copy(ref, ref, sem).wait()

    barrier = pltpu.get_barrier_semaphore()
    total = N * N * N

    def greet(i, _):
        xx, yy, zz = up(x, i // (N * N)), up(y, (i // N) % N), up(z, i % N)
        pl.semaphore_signal(
            barrier, inc=1, device_id=dev(xx, yy, zz, c), device_id_type=MESH
        )
        return _

    lax.fori_loop(1, total, greet, 0)
    for d in range(N):
        pl.semaphore_signal(
            barrier, inc=1, device_id=dev(x, up(y, d), z, other), device_id_type=MESH
        )
    for d in range(1, N):
        pl.semaphore_signal(
            barrier, inc=1, device_id=dev(x, y, up(z, d), other), device_id_type=MESH
        )
    pl.semaphore_wait(barrier, total - 1 + N + N - 1)

    slot_z, slot_y = 2 * z + c, 2 * y + c
    for d in range(N):
        for cc in (c, other):
            if d == 0 and cc is c:
                continue
            send(codes, cz.at[slot_z], s_cz.at[slot_z], dev(x, y, up(z, d), cc))
            send(codes, cy.at[slot_y], s_cy.at[slot_y], dev(x, up(y, d), z, cc))

    half = pgc // 2

    class Gather:
        def __init__(self, k, hbm, at, row, n, i1, i2, dev1, dev2):
            self.k, self.at, self.row, self.n = k, at, row, n
            self.i1, self.i2, self.dev1, self.dev2 = i1, i2, dev1, dev2
            self.own = hbm.at[0, pl.ds(row, n)]

        def first(self):
            for d in (1, 3, 2):
                send(
                    self.own,
                    self.at(self.i1, self.i2, self.row, self.n),
                    s_a.at[self.k, self.i1],
                    self.dev1(up(self.i1, d)),
                )

        def second(self, d):
            j = up(self.i1, d)
            src = self.own
            land = self.at(j, self.i2, self.row, self.n)
            if d:
                arrived(land, s_a.at[self.k, j])
                src = land
            send(src, land, s_p.at[self.k, j, 0], self.dev2(up(self.i2, 1)))
            send(src, land, s_p.at[self.k, j, 1], self.dev2(up(self.i2, 3)))

        def relay(self, d):
            j = up(self.i1, d)
            h = self.n // 2
            left, right = up(self.i2, 3), up(self.i2, 1)
            arrived(self.at(j, left, self.row, self.n), s_p.at[self.k, j, 0])
            piece = self.at(j, left, self.row, h)
            send(piece, piece, s_p.at[self.k, j, 2], self.dev2(right))
            arrived(self.at(j, right, self.row, self.n), s_p.at[self.k, j, 1])
            piece = self.at(j, right, self.row + h, h)
            send(piece, piece, s_p.at[self.k, j, 3], self.dev2(left))

        def last(self, d):
            j = up(self.i1, d)
            h = self.n // 2
            far = up(self.i2, 2)
            arrived(self.at(j, far, self.row, h), s_p.at[self.k, j, 2])
            arrived(self.at(j, far, self.row + h, h), s_p.at[self.k, j, 3])

    along_x = lambda j: dev(j, y, z, c)
    along_y = lambda j: dev(x, j, z, c)
    along_z = lambda j: dev(x, y, j, c)
    gb0 = Gather(
        0, gbs, lambda j1, j2, r, n: gb.at[j1, j2, pl.ds(r, n)], 0, half, x, y, along_x, along_y
    )
    gb1 = Gather(
        1, gbs, lambda j1, j2, r, n: gb.at[j2, j1, pl.ds(r, n)], half, half, y, x, along_y, along_x
    )
    ibz = Gather(
        2, ibs, lambda j1, j2, r, n: ib.at[j2, j1, pl.ds(r, n)], 0, pa, z, x, along_z, along_x
    )

    gb0.first()
    gb1.first()
    ibz.first()

    def grad_part(b, zz, k):
        return grad.at[b, 0, :, pl.ds(pl.multiple_of((k * N + zz) * pgc, pgc), pgc)]

    def act_part(b, yy):
        return act.at[b, 0, :, pl.ds(pl.multiple_of(yy * ga, ga), ga)]

    def gx_part(b, k):
        return gx.at[slot_z, b, :, pl.ds(k * pgc, pgc)]

    def send_grad(b, d):
        for k in range(N):
            send(
                grad_part(b, up(z, d), k), gx_part(b, k), s_gx.at[b, slot_z], along_z(up(z, d))
            )

    def send_act(b, d):
        send(act_part(b, up(y, d)), ix.at[slot_y, b], s_ix.at[b, slot_y], along_y(up(y, d)))

    def own_rows(b):
        for k in range(N):
            pltpu.make_async_copy(grad_part(b, z, k), gx_part(b, k), s_loc.at[b]).start()
            send(grad_part(b, z, k), gx_part(b, k), s_gx.at[b, slot_z], dev(x, y, z, other))
        pltpu.make_async_copy(act_part(b, y), ix.at[slot_y, b], s_loc.at[2 + b]).start()
        send(act_part(b, y), ix.at[slot_y, b], s_ix.at[b, slot_y], dev(x, y, z, other))

    for d in (1, 3, 2):
        send_act(0, d)
    for d in (1, 3, 2):
        send_grad(0, d)
    own_rows(0)
    pltpu.make_async_copy(gbs.at[0], gb.at[x, y], s_loc.at[4]).start()
    pltpu.make_async_copy(ibs.at[0], ib.at[x, z], s_loc.at[5]).start()
    cz[slot_z] = codes[...]
    cy[slot_y] = codes[...]
    for d in (1, 3, 2):
        send_grad(1, d)
    own_rows(1)

    for d in range(N):
        gb0.second(d)
        gb1.second(d)
        ibz.second(d)
    for d in (1, 3, 2):
        send_act(1, d)

    for d in range(N):
        for cc in (c, other):
            if d == 0 and cc is c:
                continue
            sz, sy = 2 * up(z, d) + cc, 2 * up(y, d) + cc
            arrived(cz.at[sz], s_cz.at[sz])
            arrived(cy.at[sy], s_cy.at[sy])

    def hand_on(buf, sem, b, q):
        s = 2 * q + c
        arrived(buf.at[s, b], sem.at[b, s])
        send(buf.at[s, b], buf.at[s, b], sem.at[b, s], dev(x, y, z, other))

    slots = N * PAIR

    def pack(buf, sem, code, dst, b, q, chunk):
        s = 2 * q + other
        arrived(buf.at[s, b], sem.at[b, s])
        numbers = code[2 * q, b : b + 1, : 2 * toks] + code[2 * q + 1, b : b + 1, : 2 * toks]
        mine = lax.broadcasted_iota(jnp.int32, (slots, 2 * toks), 0) + (1 + c * TAG)
        place = jnp.where(numbers == mine, 1.0, 0.0).astype(BF16)

        def step(i, _):
            cols = pl.ds(pl.multiple_of(i * chunk, chunk), chunk)
            block = buf[pl.ds(2 * q, 2), b, :, cols].reshape(2 * toks, chunk)
            packed = jnp.dot(place, block, preferred_element_type=F32).astype(BF16)
            dst[b, :, q, :, cols] = packed.reshape(N, PAIR, chunk)
            return _

        lax.fori_loop(0, buf.shape[3] // chunk, step, 0)

    def pack_grad(b, q):
        pack(gx, s_gx, cz, pg, b, q, 512)

    def pack_act(b, q):
        pack(ix, s_ix, cy, pi, b, q, 512)

    def local_rows(b):
        for k in range(N):
            arrived(gx_part(b, k), s_loc.at[b])
        arrived(ix.at[slot_y, b], s_loc.at[2 + b])

    local_rows(0)
    for d in (1, 3, 2):
        hand_on(ix, s_ix, 0, up(y, d))
    for d in (1, 3):
        hand_on(gx, s_gx, 0, up(z, d))
    for d in (0, 1, 3, 2):
        pack_act(0, up(y, d))
    for d in (0, 1, 3):
        pack_grad(0, up(z, d))
    for d in (0, 1):
        gb0.relay(d)
        gb1.relay(d)
        ibz.relay(d)
    hand_on(gx, s_gx, 0, up(z, 2))
    for d in (2, 3):
        gb0.relay(d)
        gb1.relay(d)
        ibz.relay(d)
    pack_grad(0, up(z, 2))
    local_rows(1)
    for d in (1, 3):
        hand_on(gx, s_gx, 1, up(z, d))
    for d in (0, 1, 3):
        pack_grad(1, up(z, d))
    for d in (1, 3, 2):
        hand_on(ix, s_ix, 1, up(y, d))
    for d in (0, 1, 3, 2):
        pack_act(1, up(y, d))
    arrived(gb.at[x, y], s_loc.at[4])
    arrived(ib.at[x, z], s_loc.at[5])
    for d in range(N):
        gb0.last(d)
        gb1.last(d)
        ibz.last(d)

    def rotate(b):
        def one(k, _):
            t = jnp.zeros((slots, ka), F32)
            for j in range(N):
                block = pi[b, k, :, :, j * pa : (j + 1) * pa].reshape(slots, pa)
                t += jnp.dot(block, ib[k, j], preferred_element_type=F32)
            io[b, k] = t.astype(BF16)
            return _

        lax.fori_loop(0, N, one, 0)

        for d in (1, 3, 2):
            k = up(y, d)
            send(io.at[b, k], ri.at[b, y], s_ri.at[b, y], along_y(k))

        def two(k, _):
            t = jnp.zeros((slots, kg), F32)
            for j in range(N):
                block = pg[b, k, :, :, j * pgc : (j + 1) * pgc].reshape(slots, pgc)
                t += jnp.dot(block, gb[k, j], preferred_element_type=F32)
            go[b, k] = t.astype(BF16)
            return _

        lax.fori_loop(0, N, two, 0)

        for d in (1, 3, 2):
            k = up(z, d)
            send(go.at[b, k], rg.at[b, z], s_rg.at[b, z], along_z(k))

    stays = y == z

    def owners(b):
        t = io[b, y].astype(F32)
        for d in (1, 3, 2):
            k = up(y, d)
            arrived(ri.at[b, k], s_ri.at[b, k])
            t += ri[b, k].astype(F32)
        rs[b] = t.astype(BF16).reshape(N, PAIR, ka)
        for d in (1, 3, 2, 0):
            k = up(y, d)
            send(
                rs.at[b, k],
                ra.at[b, z],
                s_ra.at[b, z],
                dev(x, k, y, c),
                when=None if d else jnp.logical_not(stays),
            )

        @pl.when(stays)
        def _():
            ra[b, z] = rs[b, y]

    def contract(b):
        t = go[b, z].astype(F32)
        for d in (1, 3, 2):
            k = up(z, d)
            arrived(rg.at[b, k], s_rg.at[b, k])
            t += rg[b, k].astype(F32)
        rg[b, z] = t.astype(BF16)

        for d in range(N):
            k = up(z, d)
            if d == 0:
                pl.when(jnp.logical_not(stays))(lambda: arrived(ra.at[b, k], s_ra.at[b, k]))
            else:
                arrived(ra.at[b, k], s_ra.at[b, k])

        def one(k, _):
            numbers = cz[2 * k, b : b + 1, : 2 * toks] + cz[2 * k + 1, b : b + 1, : 2 * toks]
            labels = (
                cz[2 * k, 2 + b : 3 + b, : 2 * toks] + cz[2 * k + 1, 2 + b : 3 + b, : 2 * toks]
            )
            mine = lax.broadcasted_iota(jnp.int32, (PAIR, 2 * toks), 0) + (
                1 + c * TAG + z * PAIR
            )
            label = jnp.sum(jnp.where(numbers == mine, labels, 0), axis=1, keepdims=True)
            left = ra[b, k].astype(F32).T.astype(BF16)
            right = rg[b, z, pl.ds(pl.multiple_of(k * PAIR, PAIR), PAIR), :].astype(F32)
            for r in range(0, ka, 96):
                rows_of = left[r : r + 96]
                t = jnp.zeros((96, kg), F32)
                for g in range(1, 2 * SEQS + 1):
                    masked = jnp.where(label == g, right, 0.0).astype(BF16)
                    o = jnp.dot(rows_of, masked, preferred_element_type=F32)
                    t += o * o
                acc[r // rows : (r + 96) // rows] += t.reshape(96 // rows, rows, kg)
            return _

        lax.fori_loop(0, N, one, 0)

    acc[...] = jnp.zeros_like(acc)
    rotate(0)
    hand_on(gx, s_gx, 1, up(z, 2))
    owners(0)
    pack_grad(1, up(z, 2))
    rotate(1)
    contract(0)
    owners(1)
    contract(1)

    here = x == z
    mine = N * x + y
    for dy in range(N):
        for dz in range(N):
            yy, zz = up(y, dy), up(z, dz)
            send(
                acc.at[N * yy + zz],
                fr.at[mine],
                s_fr.at[mine],
                dev(z, yy, zz, c),
                when=None if dy or dz else jnp.logical_not(here),
            )

    @pl.when(here)
    def _():
        fr[mine] = acc[p]

    t = jnp.zeros((rows, kg), F32)
    for dx in range(N):
        for dy in range(N):
            k = N * up(x, dx) + up(y, dy)
            if dx or dy:
                arrived(fr.at[k], s_fr.at[k])
            else:
                pl.when(jnp.logical_not(here))(lambda: arrived(fr.at[k], s_fr.at[k]))
    for k in range(N * N):
        t += fr[k]
    out[...] = t * (1.0 / (2 * 128 * SEQS))

    for copy, when in sends:
        if when is None:
            copy.wait_send()
        else:
            pl.when(when)(lambda copy=copy: copy.wait_send())


def slot_numbers(ids, seqs):
    toks = ids.shape[1]
    c = lax.axis_index("expert") % 2
    order = jnp.arange(toks, dtype=jnp.int32)
    earlier = (ids[:, :, None] == ids[:, None, :]) & (order[None, :] < order[:, None])[None]
    offset = jnp.sum(earlier.astype(jnp.int32), axis=2)
    number = (ids % 2) * TAG + (ids // 2) * PAIR + offset + 1 + c * CAP
    label = seqs + 1 + SEQS * c
    both = jnp.concatenate([number, label], axis=0)
    width = 256
    first = jnp.pad(both, ((0, 4), (0, width - toks)))
    second = jnp.pad(both, ((0, 4), (toks, width - 2 * toks)))
    return jnp.where(c == 0, first, second)


def per_device(activations, gradients, expert_ids, sequence_ids, input_basis, output_basis):
    micro, _, toks, wa = activations.shape
    wg = gradients.shape[3]
    pa, ka = input_basis.shape[1:]
    pgc, kg = output_basis.shape[1:]
    rows = ka // (N * N)
    codes = slot_numbers(expert_ids[:, 0, :, 0], sequence_ids[:, 0])
    slots = N * PAIR
    vmem = pltpu.VMEM
    dma = pltpu.SemaphoreType.DMA
    anywhere = pl.BlockSpec(memory_space=pl.ANY)
    return pl.pallas_call(
        functools.partial(kernel, (toks, wa, wg, ka, kg, rows)),
        out_shape=jax.ShapeDtypeStruct((rows, kg), F32),
        in_specs=[pl.BlockSpec(memory_space=vmem)] + [anywhere] * 4,
        out_specs=pl.BlockSpec(memory_space=vmem),
        scratch_shapes=[
            vmem((2 * N, 8, 256), jnp.int32),
            vmem((2 * N, 8, 256), jnp.int32),
            vmem((2 * N, micro, toks, wg // N), BF16),
            vmem((2 * N, micro, toks, wa // N), BF16),
            vmem((N, N, pgc, kg), BF16),
            vmem((N, N, pa, ka), BF16),
            vmem((micro, N, N, PAIR, wg // N), BF16),
            vmem((micro, N, N, PAIR, wa // N), BF16),
            vmem((micro, N, slots, kg), BF16),
            vmem((micro, N, slots, ka), BF16),
            vmem((micro, N, slots, kg), BF16),
            vmem((micro, N, slots, ka), BF16),
            vmem((micro, N, PAIR, ka), BF16),
            vmem((micro, N, PAIR, ka), BF16),
            vmem((N * N, rows, kg), F32),
            vmem((N * N, rows, kg), F32),
            dma((192,)),
            dma((2 * N,)),
            dma((2 * N,)),
            dma((micro, 2 * N)),
            dma((micro, 2 * N)),
            dma((6,)),
            dma((3, N)),
            dma((3, N, 4)),
            dma((micro, N)),
            dma((micro, N)),
            dma((micro, N)),
            dma((N * N,)),
        ],
        compiler_params=pltpu.CompilerParams(
            collective_id=0, has_side_effects=True, vmem_limit_bytes=63 << 20
        ),
        name="eigen",
    )(codes, activations, gradients, input_basis, output_basis)[None]


def solution(mesh):
    placed = (
        P(None, ("expert", "panel"), None, None),
        P(None, ("expert", "panel"), None, None),
        P(None, ("expert", "panel"), None, None),
        P(None, ("expert", "panel"), None),
        P("expert", "panel", None),
        P("expert", "panel", None),
    )
    return jax.shard_map(
        per_device,
        mesh=mesh,
        in_specs=placed,
        out_specs=P("expert", "panel", None),
        check_vma=False,
    )
```

time: 331 us -> 149 us (0.45)
  waiting for transfers between devices: 147 us -> 0 us
  Pallas kernels: 0 us -> 143 us
  local copies, waits for them, and re-layouts: 70.1 us -> 1.35 us
  other arithmetic: 35.6 us -> 3.01 us
  starting transfers between devices: 28.1 us -> 0 us
  matrix products: 17.9 us -> 0 us
  blocking collectives: 16.9 us -> 0 us
  between operations: 13.6 us -> 0.02 us
    all_to_all x6 -> x0, waiting for transfers between devices: 146 us -> none  [the longest x2 118 us: receive_rows(): lax.all_to_all(packed[1], 'expert', split_axis=0, concat_axis=0, tiled=True)]
    pallas_call x0 -> x1, Pallas kernels: none -> 143 us  [per_device(): pl.pallas_call(functools.partial(kernel, (toks, wa, wg, ka, kg, rows)), o...]
    gather x10 -> x0, local copies, waits for them, and re-layouts: 44.8 us -> none  [the longest x4 28.2 us: pack_rows(): grads[source]]
    all_to_all x6 -> x0, starting transfers between devices: 28.1 us -> none  [the longest x2 9.82 us: receive_rows(): lax.all_to_all(packed[1], 'expert', split_axis=0, concat_axis=0, tiled=True)]
    dot_general x3 -> x0, matrix products: 17.9 us -> none  [the longest x1 8.66 us: rotate_rows(): jnp.dot(columns, lax.all_gather(output_basis[0], 'panel', axis=0, tiled=T...]
    all_to_all x1 -> x0, blocking collectives: 16.9 us -> none  [sent_and_summed(): lax.all_to_all(pieces, axis, split_axis=0, concat_axis=0, tiled=True)]
    select_n x8 -> x1, other arithmetic: 17 us -> 0.68 us  [slot_numbers(): return jnp.where(c == 0, first, second)]
    concatenate x3 -> x1, other arithmetic: 16.1 us -> 0.01 us  [slot_numbers(): both = jnp.concatenate([number, label], axis=0)]
  transfers between devices with their start and end apart: 8 -> 0, of which waited for: 4 -> 0; matrix products, arithmetic and copies ran while one was open for 33% -> 0% of each run, Pallas kernels for 0% -> 0%
where the time goes in v1:
time: 149 us; the launch traced here: 148 us
  Pallas kernels  143 us (96%)
  other arithmetic  3.01 us (2%)
    pallas_call x1, Pallas kernels, per_device(): pl.pallas_call(functools.partial(kernel, (toks, wa, wg, ka, kg, rows)), o...  143 us

profile of v1, /device:TPU:0, one launch (start us, length us, event | category | flops | bytes accessed | tf_op | source)
XLA Modules:
  0.0 147.8 jit_solution(10869969699812586868)
XLA Ops:
  0.0 0.7 add_bitcast_fusion
  0.7 0.9 convert_reduce_fusion
  1.6 0.7 add_add_fusion
  2.3 0.7 pad_select_fusion.refs_0_
  3.0 143.4 %eigen.1 = f32[24,256]{1,0:T(8,128)} custom-call(s32[8,256]{1,0:T(8,128)} %pad_select_fusion.refs_0_, bf16[2,1,96,6144]{3,2,1,0:T(8,128)(2,1)} %refs_1_.1, bf16[2,1,96,16384]{3,2,1,0:T(8,128)(2,1)} %refs_2_.1, bf16[1,384,384]{2,1,0:T(8,128)(2,1)} %refs_3_.1, bf16[1,1024,256]{2,1,0:T(8,128)(2,1)} %refs_4_.1), custom_call_target="tpu_custom_call" | custom-call | tf_op jit(solution)/shard_map/eigen/pallas_call | solution.py:435
  146.5 1.3 copy.10
  (2 shorter events, 0.0 us)

commit v2 on v1

v2 whole, which is shorter than its diff:
```python
import functools

import jax
import jax.numpy as jnp
from jax import lax
from jax.experimental import pallas as pl
from jax.experimental.pallas import tpu as pltpu
from jax.sharding import PartitionSpec as P

MESH = pl.DeviceIdType.MESH
SEQS = 4
N = 4
CAP = 18
PAIR = 48
NEAR = (0, 1, 3, 2)
TAG = 1024
BF16 = jnp.bfloat16
F32 = jnp.float32


def kernel(sizes, *refs):
    (ids, seqs, act, grad, ibs, gbs, out) = refs[:7]
    (lanes, codes, cz, cy, gx, ix, gb, ib, pg, pi, go, io, rg, ri, rs, ra, acc, fr) = refs[7:25]
    (s_send, s_cz, s_cy, s_gx, s_ix, s_loc, s_a, s_f, s_p, s_rg, s_ri, s_ra, s_fr) = refs[25:]
    toks, wa, wg, ka, kg, rows = sizes
    ga, gg = wa // N, wg // N
    pa, pgc = ga // N, gg // N
    e = lax.axis_index("expert")
    p = lax.axis_index("panel")
    x, c = e // 2, e % 2
    y, z = p // N, p % N
    other = 1 - c

    def dev(xx, yy, zz, cc):
        return (2 * xx + cc, N * yy + zz)

    def up(i, d):
        return (i + d) % N

    sends = []

    def send(src, dst, sem, device, when=None):
        i = len(sends)
        copy = pltpu.make_async_remote_copy(
            src_ref=src,
            dst_ref=dst,
            send_sem=s_send.at[i],
            recv_sem=sem,
            device_id=device,
            device_id_type=MESH,
        )
        sends.append((copy, when))
        if when is None:
            copy.start()
        else:
            pl.when(when)(lambda: copy.start())

    def sent(some):
        for copy, when in some:
            if when is None:
                copy.wait_send()
            else:
                pl.when(when)(lambda copy=copy: copy.wait_send())

    def arrived(ref, sem):
        pltpu.make_async_copy(ref, ref, sem).wait()

    held = up(z, N - x)
    here = x == held
    barrier = pltpu.get_barrier_semaphore()

    def greet(*device):
        pl.semaphore_signal(barrier, inc=1, device_id=dev(*device), device_id_type=MESH)

    xs, ys, zs = ([up(i, d) for d in range(N)] for i in (x, y, z))
    for d in range(1, N):
        greet(x, ys[d], z, other)
        greet(x, y, zs[d], other)
    greet(x, y, z, other)
    for dx in (2, 1, 3, 0):
        for dy in (2, 1, 3, 0):
            for dz in (2, 1, 3, 0):
                if dx or dy or dz:
                    greet(xs[dx], ys[dy], zs[dz], c)

    codes[...] = jnp.zeros_like(codes)
    lanes[...] = jnp.full_like(lanes, -1.0)
    above = lax.broadcasted_iota(jnp.int32, (2 * toks, 2 * toks), 0) < lax.broadcasted_iota(
        jnp.int32, (2 * toks, 2 * toks), 1
    )
    for b in range(2):
        for cc in range(2):

            @pl.when(c == cc)
            def _():
                lanes[b : b + 1, cc * toks : (cc + 1) * toks] = ids[b].astype(F32)

        row = lanes[b : b + 1, : 2 * toks]
        column = jnp.broadcast_to(row, (8, 2 * toks)).T[:, :1]
        earlier = jnp.logical_and(column == row, above)
        offset = jnp.sum(jnp.where(earlier, 1.0, 0.0), axis=0, keepdims=True).astype(jnp.int32)
        expert = row.astype(jnp.int32)
        number = (expert & 1) * TAG + (expert >> 1) * PAIR + offset + (1 + c * CAP)
        codes[b : b + 1, : 2 * toks] = jnp.where(expert < 0, 0, number)
    for cc in range(2):

        @pl.when(c == cc)
        def _():
            codes[2:4, cc * toks : (cc + 1) * toks] = seqs[:, 0] + (1 + SEQS * cc)

    pl.semaphore_wait(barrier, N * N * N + 2 * (N - 1))

    slot_z, slot_y = 2 * z + c, 2 * y + c
    for d in range(N):
        for cc in (c, other):
            if d == 0 and cc is c:
                continue
            send(codes, cz.at[slot_z], s_cz.at[slot_z], dev(x, y, up(z, d), cc))
            send(codes, cy.at[slot_y], s_cy.at[slot_y], dev(x, up(y, d), z, cc))

    cut = pgc * 5 // 8

    class Gather:
        def __init__(self, k, hbm, at, row, n, i1, i2, dev1, dev2, direct):
            self.direct = direct
            self.k, self.at, self.row, self.n = k, at, row, n
            self.i1, self.i2, self.dev1, self.dev2 = i1, i2, dev1, dev2
            self.own = hbm.at[0, pl.ds(row, n)]

        def first(self):
            for d in (1, 3, 2) if self.direct else (1, 3):
                send(
                    self.own,
                    self.at(self.i1, self.i2, self.row, self.n),
                    s_a.at[self.k, self.i1],
                    self.dev1(up(self.i1, d)),
                )

        def first_relay(self):
            h = self.n // 2
            for d, row in ((3, self.row), (1, self.row + h)):
                j = up(self.i1, d)
                arrived(self.at(j, self.i2, self.row, self.n), s_a.at[self.k, j])
                piece = self.at(j, self.i2, row, h)
                send(piece, piece, s_f.at[self.k, d // 2], self.dev1(up(self.i1, N - d)))

        def second(self, d):
            j = up(self.i1, d)
            land = self.at(j, self.i2, self.row, self.n)
            src = land if d else self.own
            if d and (self.direct or d != 2):
                if self.direct:
                    arrived(land, s_a.at[self.k, j])
            elif d:
                h = self.n // 2
                arrived(self.at(j, self.i2, self.row, h), s_f.at[self.k, 1])
                arrived(self.at(j, self.i2, self.row + h, h), s_f.at[self.k, 0])
            send(src, land, s_p.at[self.k, j, 0], self.dev2(up(self.i2, 1)))
            send(src, land, s_p.at[self.k, j, 1], self.dev2(up(self.i2, 3)))

        def relay(self, d):
            j = up(self.i1, d)
            h = self.n // 2
            left, right = up(self.i2, 3), up(self.i2, 1)
            arrived(self.at(j, left, self.row, self.n), s_p.at[self.k, j, 0])
            piece = self.at(j, left, self.row, h)
            send(piece, piece, s_p.at[self.k, j, 2], self.dev2(right))
            arrived(self.at(j, right, self.row, self.n), s_p.at[self.k, j, 1])
            piece = self.at(j, right, self.row + h, h)
            send(piece, piece, s_p.at[self.k, j, 3], self.dev2(left))

        def last(self, d):
            j = up(self.i1, d)
            h = self.n // 2
            far = up(self.i2, 2)
            arrived(self.at(j, far, self.row, h), s_p.at[self.k, j, 2])
            arrived(self.at(j, far, self.row + h, h), s_p.at[self.k, j, 3])

    along_x = lambda j: dev(j, y, z, c)
    along_y = lambda j: dev(x, j, z, c)
    along_z = lambda j: dev(x, y, j, c)
    gb0 = Gather(
        0, gbs, lambda j1, j2, r, n: gb.at[j1, j2, pl.ds(r, n)], 0, cut, x, y, along_x, along_y, False
    )
    gb1 = Gather(
        1, gbs, lambda j1, j2, r, n: gb.at[j2, j1, pl.ds(r, n)], cut, pgc - cut, y, x, along_y, along_x, False
    )
    ibz = Gather(
        2, ibs, lambda j1, j2, r, n: ib.at[j2, j1, pl.ds(r, n)], 0, pa, z, x, along_z, along_x, True
    )

    gb0.first()
    gb1.first()
    ibz.first()

    def grad_part(b, zz, k):
        return grad.at[b, 0, :, pl.ds(pl.multiple_of((k * N + zz) * pgc, pgc), pgc)]

    def act_part(b, yy):
        return act.at[b, 0, :, pl.ds(pl.multiple_of(yy * ga, ga), ga)]

    def gx_part(b, k):
        return gx.at[slot_z, b, :, pl.ds(k * pgc, pgc)]

    def send_grad(b, d):
        for k in range(N):
            send(
                grad_part(b, up(z, d), k), gx_part(b, k), s_gx.at[b, slot_z], along_z(up(z, d))
            )

    def send_act(b, d):
        send(act_part(b, up(y, d)), ix.at[slot_y, b], s_ix.at[b, slot_y], along_y(up(y, d)))

    def own_rows(b):
        for k in range(N):
            pltpu.make_async_copy(grad_part(b, z, k), gx_part(b, k), s_loc.at[b]).start()
            send(grad_part(b, z, k), gx_part(b, k), s_gx.at[b, slot_z], dev(x, y, z, other))
        pltpu.make_async_copy(act_part(b, y), ix.at[slot_y, b], s_loc.at[2 + b]).start()
        send(act_part(b, y), ix.at[slot_y, b], s_ix.at[b, slot_y], dev(x, y, z, other))

    for d in (1, 3, 2):
        send_grad(0, d)
    ibz.second(0)
    gb0.second(0)
    gb0.first_relay()
    gb1.first_relay()
    for d in (1, 3, 2):
        send_act(0, d)
    gb1.second(0)
    own_rows(0)
    pltpu.make_async_copy(gbs.at[0], gb.at[x, y], s_loc.at[4]).start()
    pltpu.make_async_copy(ibs.at[0], ib.at[x, z], s_loc.at[5]).start()
    cz[slot_z] = codes[...]
    cy[slot_y] = codes[...]
    for d in (1, 3, 2):
        send_grad(1, d)
    own_rows(1)

    for d in (1, 3, 2):
        ibz.second(d)
        gb0.second(d)
    for d in (1, 3, 2):
        gb1.second(d)
    for d in (1, 3, 2):
        send_act(1, d)

    for d in range(N):
        for cc in (c, other):
            if d == 0 and cc is c:
                continue
            sz, sy = 2 * up(z, d) + cc, 2 * up(y, d) + cc
            arrived(cz.at[sz], s_cz.at[sz])
            arrived(cy.at[sy], s_cy.at[sy])

    def hand_on(buf, sem, b, q):
        s = 2 * q + c
        arrived(buf.at[s, b], sem.at[b, s])
        send(buf.at[s, b], buf.at[s, b], sem.at[b, s], dev(x, y, z, other))

    slots = N * PAIR

    def pack(buf, sem, code, dst, b, q, pos, chunk):
        s = 2 * q + other
        arrived(buf.at[s, b], sem.at[b, s])
        numbers = code[2 * q, b : b + 1, : 2 * toks] + code[2 * q + 1, b : b + 1, : 2 * toks]
        mine = lax.broadcasted_iota(jnp.int32, (slots, 2 * toks), 0) + (1 + c * TAG)
        place = jnp.where(numbers == mine, 1.0, 0.0).astype(BF16)

        def step(i, _):
            cols = pl.ds(pl.multiple_of(i * chunk, chunk), chunk)
            block = buf[pl.ds(2 * q, 2), b, :, cols].reshape(2 * toks, chunk)
            packed = jnp.dot(place, block, preferred_element_type=F32).astype(BF16)
            dst[b, :, pos, :, cols] = packed.reshape(N, PAIR, chunk)
            return _

        lax.fori_loop(0, buf.shape[3] // chunk, step, 0)

    def pack_grad(b, d):
        pack(gx, s_gx, cz, pg, b, up(z, d), NEAR.index(d), 512)

    def pack_act(b, d):
        pack(ix, s_ix, cy, pi, b, up(y, d), NEAR.index(d), 512)

    def local_rows(b):
        for k in range(N):
            arrived(gx_part(b, k), s_loc.at[b])
        arrived(ix.at[slot_y, b], s_loc.at[2 + b])

    def rotate(src, basis, dst, b, k, lo, hi):
        depth = basis.shape[2]
        m = (hi - lo) * PAIR
        t = jnp.zeros((m, basis.shape[3]), F32)
        for j in range(N):
            block = src[b, k, lo:hi, :, j * depth : (j + 1) * depth].reshape(m, depth)
            t += jnp.dot(block, basis[k, j], preferred_element_type=F32)
        dst[b, k, lo:hi] = t.astype(BF16).reshape(hi - lo, PAIR, basis.shape[3])

    def rotate_in(b, experts):
        for d in experts:
            rotate(pi, ib, io, b, up(x, d), 0, N)

    def rotate_out(b, experts, lo, hi):
        for d in experts:
            rotate(pg, gb, go, b, up(x, d), lo, hi)

    def share(src, dst, sem, me, along, b, experts, lo, hi):
        for d in experts:
            k = up(x, d)
            owner = (k + x) % N
            for i in range(lo, hi):
                send(
                    src.at[b, k, i],
                    dst.at[b, me, up(me, NEAR[i])],
                    sem.at[b, me],
                    along(owner),
                    when=owner != me,
                )

    def share_in(b, experts):
        share(io, ri, s_ri, y, along_y, b, experts, 0, N)

    def share_out(b, experts, lo, hi):
        share(go, rg, s_rg, z, along_z, b, experts, lo, hi)

    close, far = NEAR[:3], NEAR[3:]

    local_rows(0)
    for d in (1, 3, 2):
        hand_on(ix, s_ix, 0, up(y, d))
    for d in (1, 3):
        hand_on(gx, s_gx, 0, up(z, d))
    for d in NEAR:
        pack_act(0, d)
    arrived(ib.at[x, z], s_loc.at[5])
    for d in close:
        pack_grad(0, d)
    for d in NEAR:
        ibz.relay(d)
    rotate_in(0, close)
    share_in(0, close)
    hand_on(gx, s_gx, 0, up(z, 2))
    for d in NEAR:
        gb0.relay(d)
    pack_grad(0, 2)
    local_rows(1)
    for d in (1, 3, 2):
        hand_on(ix, s_ix, 1, up(y, d))
    for d in NEAR:
        gb1.relay(d)
    for d in NEAR:
        pack_act(1, d)
    rotate_in(1, close)
    share_in(1, close)
    for d in (1, 3):
        hand_on(gx, s_gx, 1, up(z, d))
    for d in close:
        pack_grad(1, d)
    for d in NEAR:
        ibz.last(d)
    for b in range(2):
        rotate_in(b, far)
        share_in(b, far)
    arrived(gb.at[x, y], s_loc.at[4])
    for d in close:
        gb0.last(d)
        rotate_out(0, (d,), 0, N)
        rotate_out(1, (d,), 0, 3)
        share_out(0, (d,), 0, N)
        share_out(1, (d,), 0, 3)
    gb0.last(2)
    for d in range(N):
        gb1.last(d)
    rotate_out(0, far, 0, N)
    rotate_out(1, far, 0, 3)
    share_out(0, far, 0, N)
    share_out(1, far, 0, 3)
    hand_on(gx, s_gx, 1, up(z, 2))
    pack_grad(1, 2)
    rotate_out(1, NEAR, 3, N)
    share_out(1, NEAR, 3, N)

    def owned(src, dst, sem, me, b, store):
        for d in (1, 3, 2):
            k = up(me, d)
            arrived(dst.at[b, k], sem.at[b, k])
        for i, d in enumerate(NEAR):
            q = up(me, d)
            t = src[b, up(me, N - x), i].astype(F32)
            for j in (1, 3, 2):
                t += dst[b, up(me, j), q].astype(F32)
            store(q, t.astype(BF16))

    stays = y == z

    def owners(b):
        def store(q, value):
            rs[b, q] = value

        owned(io, ri, s_ri, y, b, store)
        for d in (1, 3, 2, 0):
            k = up(y, d)
            send(
                rs.at[b, k],
                ra.at[b, z],
                s_ra.at[b, z],
                dev(x, k, y, c),
                when=None if d else jnp.logical_not(stays),
            )

        @pl.when(stays)
        def _():
            ra[b, z] = rs[b, y]

    def contract(b):
        def store(q, value):
            rg[b, z, q] = value

        owned(go, rg, s_rg, z, b, store)
        for d in range(N):
            k = up(z, d)
            if d == 0:
                pl.when(jnp.logical_not(stays))(lambda: arrived(ra.at[b, k], s_ra.at[b, k]))
            else:
                arrived(ra.at[b, k], s_ra.at[b, k])

        def one(k, _):
            numbers = cz[2 * k, b : b + 1, : 2 * toks] + cz[2 * k + 1, b : b + 1, : 2 * toks]
            labels = (
                cz[2 * k, 2 + b : 3 + b, : 2 * toks] + cz[2 * k + 1, 2 + b : 3 + b, : 2 * toks]
            )
            mine = lax.broadcasted_iota(jnp.int32, (PAIR, 2 * toks), 0) + (
                1 + c * TAG + up(z, N - x) * PAIR
            )
            label = jnp.sum(jnp.where(numbers == mine, labels, 0), axis=1, keepdims=True)
            left = ra[b, k].astype(F32).T.astype(BF16)
            right = rg[b, z, k].astype(F32)
            for r in range(0, ka, 96):
                rows_of = left[r : r + 96]
                t = jnp.zeros((96, kg), F32)
                for g in range(1, 2 * SEQS + 1):
                    masked = jnp.where(label == g, right, 0.0).astype(BF16)
                    o = jnp.dot(rows_of, masked, preferred_element_type=F32)
                    t += o * o
                acc[r // rows : (r + 96) // rows] += t.reshape(96 // rows, rows, kg)
            return _

        lax.fori_loop(0, N, one, 0)

    acc[...] = jnp.zeros_like(acc)
    for b in range(2):
        owners(b)
    for b in range(2):
        contract(b)

    early = len(sends)

    mine = N * x + y
    for dy in range(N):
        for dz in range(N):
            yy, zz = up(y, dy), up(z, dz)
            send(
                acc.at[N * yy + zz],
                fr.at[mine],
                s_fr.at[mine],
                dev(held, yy, zz, c),
                when=None if dy or dz else jnp.logical_not(here),
            )

    @pl.when(here)
    def _():
        fr[mine] = acc[p]

    sent(sends[:early])
    t = jnp.zeros((rows, kg), F32)
    for dx in range(N):
        for dy in range(N):
            k = N * up(x, dx) + up(y, dy)
            if dx or dy:
                arrived(fr.at[k], s_fr.at[k])
            else:
                pl.when(jnp.logical_not(here))(lambda: arrived(fr.at[k], s_fr.at[k]))
    for k in range(N * N):
        t += fr[k]
    out[...] = t * (1.0 / (2 * 128 * SEQS))

    sent(sends[early:])


def per_device(activations, gradients, expert_ids, sequence_ids, input_basis, output_basis):
    micro, _, toks, wa = activations.shape
    wg = gradients.shape[3]
    pa, ka = input_basis.shape[1:]
    pgc, kg = output_basis.shape[1:]
    rows = ka // (N * N)
    vmem = pltpu.VMEM
    dma = pltpu.SemaphoreType.DMA
    anywhere = pl.BlockSpec(memory_space=pl.ANY)
    return pl.pallas_call(
        functools.partial(kernel, (toks, wa, wg, ka, kg, rows)),
        out_shape=jax.ShapeDtypeStruct((rows, kg), F32),
        in_specs=[pl.BlockSpec(memory_space=vmem)] * 2 + [anywhere] * 4,
        out_specs=pl.BlockSpec(memory_space=vmem),
        scratch_shapes=[
            vmem((8, 256), F32),
            vmem((8, 256), jnp.int32),
            vmem((2 * N, 8, 256), jnp.int32),
            vmem((2 * N, 8, 256), jnp.int32),
            vmem((2 * N, micro, toks, wg // N), BF16),
            vmem((2 * N, micro, toks, wa // N), BF16),
            vmem((N, N, pgc, kg), BF16),
            vmem((N, N, pa, ka), BF16),
            vmem((micro, N, N, PAIR, wg // N), BF16),
            vmem((micro, N, N, PAIR, wa // N), BF16),
            vmem((micro, N, N, PAIR, kg), BF16),
            vmem((micro, N, N, PAIR, ka), BF16),
            vmem((micro, N, N, PAIR, kg), BF16),
            vmem((micro, N, N, PAIR, ka), BF16),
            vmem((micro, N, PAIR, ka), BF16),
            vmem((micro, N, PAIR, ka), BF16),
            vmem((N * N, rows, kg), F32),
            vmem((N * N, rows, kg), F32),
            dma((256,)),
            dma((2 * N,)),
            dma((2 * N,)),
            dma((micro, 2 * N)),
            dma((micro, 2 * N)),
            dma((6,)),
            dma((3, N)),
            dma((3, 2)),
            dma((3, N, 4)),
            dma((micro, N)),
            dma((micro, N)),
            dma((micro, N)),
            dma((N * N,)),
        ],
        compiler_params=pltpu.CompilerParams(
            collective_id=0, has_side_effects=True, vmem_limit_bytes=63 << 20
        ),
        name="eigen",
    )(expert_ids[..., 0], sequence_ids, activations, gradients, input_basis, output_basis)[None]


def solution(mesh):
    placed = (
        P(None, ("expert", "panel"), None, None),
        P(None, ("expert", "panel"), None, None),
        P(None, ("expert", "panel"), None, None),
        P(None, ("expert", "panel"), None),
        P("expert", "panel", None),
        P("expert", "panel", None),
    )
    return jax.shard_map(
        per_device,
        mesh=mesh,
        in_specs=placed,
        out_specs=P("expert", "panel", None),
        check_vma=False,
    )
```

time: 149 us -> 131 us (0.88)
  Pallas kernels: 143 us -> 130 us
  other arithmetic: 3.01 us -> 0 us
    pallas_call x1, Pallas kernels: 143 us -> 130 us  [per_device(): pl.pallas_call(functools.partial(kernel, (toks, wa, wg, ka, kg, rows)), o...]
where the time goes in v2:
time: 131 us
  Pallas kernels  130 us (99%)
  local copies, waits for them, and re-layouts  1.35 us (1%)
    pallas_call x1, Pallas kernels, per_device(): pl.pallas_call(functools.partial(kernel, (toks, wa, wg, ka, kg, rows)), o...  130 us

profile of v2, /device:TPU:0, one launch (start us, length us, event | category | flops | bytes accessed | tf_op | source)
XLA Modules:
  0.0 130.9 jit_solution(16242999690177844956)
XLA Ops:
  0.0 129.5 %eigen.1 = f32[24,256]{1,0:T(8,128)} custom-call(s32[2,1,96]{2,1,0:T(1,128)} %bitcast.3, s32[2,1,96]{2,1,0:T(1,128)} %refs_1_.1, bf16[2,1,96,6144]{3,2,1,0:T(8,128)(2,1)} %refs_2_.1, bf16[2,1,96,16384]{3,2,1,0:T(8,128)(2,1)} %refs_3_.1, bf16[1,384,384]{2,1,0:T(8,128)(2,1)} %refs_4_.1, bf16[1,1024,256]{2,1,0:T(8,128)(2,1)} %refs_5_.1), custom_call_target="tpu_custom_call" | custom-call | tf_op jit(solution)/shard_map/eigen/pallas_call | solution.py:498
  129.5 1.3 %copy.8 = f32[1,24,256]{2,1,0:T(8,128)} copy(f32[1,24,256]{2,1,0:T(8,128)} %bitcast.2) | data formatting | bytes 49152

commit v3 on v2

--- a/solution.py
+++ b/solution.py
@@ -37,30 +37,24 @@
     def up(i, d):
         return (i + d) % N
 
-    sends = []
-
-    def send(src, dst, sem, device, when=None):
-        i = len(sends)
+    groups = {}
+
+    def send(src, dst, sem, device, group, when=None):
         copy = pltpu.make_async_remote_copy(
             src_ref=src,
             dst_ref=dst,
-            send_sem=s_send.at[i],
+            send_sem=s_send.at[groups.setdefault(group, len(groups))],
             recv_sem=sem,
             device_id=device,
             device_id_type=MESH,
         )
-        sends.append((copy, when))
         if when is None:
             copy.start()
         else:
             pl.when(when)(lambda: copy.start())
 
-    def sent(some):
-        for copy, when in some:
-            if when is None:
-                copy.wait_send()
-            else:
-                pl.when(when)(lambda copy=copy: copy.wait_send())
+    def sent(group, size):
+        arrived(size, s_send.at[groups[group]])
 
     def arrived(ref, sem):
         pltpu.make_async_copy(ref, ref, sem).wait()
@@ -115,14 +109,15 @@
         for cc in (c, other):
             if d == 0 and cc is c:
                 continue
-            send(codes, cz.at[slot_z], s_cz.at[slot_z], dev(x, y, up(z, d), cc))
-            send(codes, cy.at[slot_y], s_cy.at[slot_y], dev(x, up(y, d), z, cc))
-
-    cut = pgc * 5 // 8
+            send(codes, cz.at[slot_z], s_cz.at[slot_z], dev(x, y, up(z, d), cc), "cz")
+            send(codes, cy.at[slot_y], s_cy.at[slot_y], dev(x, up(y, d), z, cc), "cy")
+
+    cut = pgc // 2
 
     class Gather:
-        def __init__(self, k, hbm, at, row, n, i1, i2, dev1, dev2, direct):
+        def __init__(self, k, hbm, at, row, n, i1, i2, dev1, dev2, direct, buf):
             self.direct = direct
+            self.parts = lambda a, b, r, n: buf.at[a, b, pl.ds(r, n)]
             self.k, self.at, self.row, self.n = k, at, row, n
             self.i1, self.i2, self.dev1, self.dev2 = i1, i2, dev1, dev2
             self.own = hbm.at[0, pl.ds(row, n)]
@@ -134,6 +129,7 @@
                     self.at(self.i1, self.i2, self.row, self.n),
                     s_a.at[self.k, self.i1],
                     self.dev1(up(self.i1, d)),
+                    (self.k, 1),
                 )
 
         def first_relay(self):
@@ -142,7 +138,7 @@
                 j = up(self.i1, d)
                 arrived(self.at(j, self.i2, self.row, self.n), s_a.at[self.k, j])
                 piece = self.at(j, self.i2, row, h)
-                send(piece, piece, s_f.at[self.k, d // 2], self.dev1(up(self.i1, N - d)))
+                send(piece, piece, s_f.at[self.k, d // 2], self.dev1(up(self.i1, N - d)), (self.k, 1))
 
         def second(self, d):
             j = up(self.i1, d)
@@ -155,8 +151,8 @@
                 h = self.n // 2
                 arrived(self.at(j, self.i2, self.row, h), s_f.at[self.k, 1])
                 arrived(self.at(j, self.i2, self.row + h, h), s_f.at[self.k, 0])
-            send(src, land, s_p.at[self.k, j, 0], self.dev2(up(self.i2, 1)))
-            send(src, land, s_p.at[self.k, j, 1], self.dev2(up(self.i2, 3)))
+            send(src, land, s_p.at[self.k, j, 0], self.dev2(up(self.i2, 1)), (self.k, 2))
+            send(src, land, s_p.at[self.k, j, 1], self.dev2(up(self.i2, 3)), (self.k, 2))
 
         def relay(self, d):
             j = up(self.i1, d)
@@ -164,10 +160,15 @@
             left, right = up(self.i2, 3), up(self.i2, 1)
             arrived(self.at(j, left, self.row, self.n), s_p.at[self.k, j, 0])
             piece = self.at(j, left, self.row, h)
-            send(piece, piece, s_p.at[self.k, j, 2], self.dev2(right))
+            send(piece, piece, s_p.at[self.k, j, 2], self.dev2(right), (self.k, 3))
             arrived(self.at(j, right, self.row, self.n), s_p.at[self.k, j, 1])
             piece = self.at(j, right, self.row + h, h)
-            send(piece, piece, s_p.at[self.k, j, 3], self.dev2(left))
+            send(piece, piece, s_p.at[self.k, j, 3], self.dev2(left), (self.k, 3))
+
+        def sent(self):
+            sent((self.k, 1), self.parts(slice(0, 1), slice(0, 3), self.row, self.n))
+            sent((self.k, 2), self.parts(slice(0, 2), slice(0, N), self.row, self.n))
+            sent((self.k, 3), self.parts(slice(0, 1), slice(0, N), self.row, self.n))
 
         def last(self, d):
             j = up(self.i1, d)
@@ -180,13 +181,13 @@
     along_y = lambda j: dev(x, j, z, c)
     along_z = lambda j: dev(x, y, j, c)
     gb0 = Gather(
-        0, gbs, lambda j1, j2, r, n: gb.at[j1, j2, pl.ds(r, n)], 0, cut, x, y, along_x, along_y, False
+        0, gbs, lambda j1, j2, r, n: gb.at[j1, j2, pl.ds(r, n)], 0, cut, x, y, along_x, along_y, False, gb
     )
     gb1 = Gather(
-        1, gbs, lambda j1, j2, r, n: gb.at[j2, j1, pl.ds(r, n)], cut, pgc - cut, y, x, along_y, along_x, False
+        1, gbs, lambda j1, j2, r, n: gb.at[j2, j1, pl.ds(r, n)], cut, pgc - cut, y, x, along_y, along_x, False, gb
     )
     ibz = Gather(
-        2, ibs, lambda j1, j2, r, n: ib.at[j2, j1, pl.ds(r, n)], 0, pa, z, x, along_z, along_x, True
+        2, ibs, lambda j1, j2, r, n: ib.at[j2, j1, pl.ds(r, n)], 0, pa, z, x, along_z, along_x, True, ib
     )
 
     gb0.first()
@@ -205,18 +206,30 @@
     def send_grad(b, d):
         for k in range(N):
             send(
-                grad_part(b, up(z, d), k), gx_part(b, k), s_gx.at[b, slot_z], along_z(up(z, d))
+                grad_part(b, up(z, d), k),
+                gx_part(b, k),
+                s_gx.at[b, slot_z],
+                along_z(up(z, d)),
+                ("grad", b),
             )
 
     def send_act(b, d):
-        send(act_part(b, up(y, d)), ix.at[slot_y, b], s_ix.at[b, slot_y], along_y(up(y, d)))
+        send(act_part(b, up(y, d)), ix.at[slot_y, b], s_ix.at[b, slot_y], along_y(up(y, d)), ("act", b))
 
     def own_rows(b):
         for k in range(N):
             pltpu.make_async_copy(grad_part(b, z, k), gx_part(b, k), s_loc.at[b]).start()
-            send(grad_part(b, z, k), gx_part(b, k), s_gx.at[b, slot_z], dev(x, y, z, other))
+            send(
+                grad_part(b, z, k),
+                gx_part(b, k),
+                s_gx.at[b, slot_z],
+                dev(x, y, z, other),
+                ("grad", b),
+            )
         pltpu.make_async_copy(act_part(b, y), ix.at[slot_y, b], s_loc.at[2 + b]).start()
-        send(act_part(b, y), ix.at[slot_y, b], s_ix.at[b, slot_y], dev(x, y, z, other))
+        send(
+            act_part(b, y), ix.at[slot_y, b], s_ix.at[b, slot_y], dev(x, y, z, other), ("act", b)
+        )
 
     for d in (1, 3, 2):
         send_grad(0, d)
@@ -255,7 +268,8 @@
     def hand_on(buf, sem, b, q):
         s = 2 * q + c
         arrived(buf.at[s, b], sem.at[b, s])
-        send(buf.at[s, b], buf.at[s, b], sem.at[b, s], dev(x, y, z, other))
+        group = ("on", buf is gx, b)
+        send(buf.at[s, b], buf.at[s, b], sem.at[b, s], dev(x, y, z, other), group)
 
     slots = N * PAIR
 
@@ -313,6 +327,7 @@
                     dst.at[b, me, up(me, NEAR[i])],
                     sem.at[b, me],
                     along(owner),
+                    ("share", src is io, b),
                     when=owner != me,
                 )
 
@@ -404,6 +419,7 @@
                 ra.at[b, z],
                 s_ra.at[b, z],
                 dev(x, k, y, c),
+                ("own", b, d == 0),
                 when=None if d else jnp.logical_not(stays),
             )
 
@@ -452,8 +468,6 @@
     for b in range(2):
         contract(b)
 
-    early = len(sends)
-
     mine = N * x + y
     for dy in range(N):
         for dz in range(N):
@@ -463,6 +477,7 @@
                 fr.at[mine],
                 s_fr.at[mine],
                 dev(held, yy, zz, c),
+                ("sums", not (dy or dz)),
                 when=None if dy or dz else jnp.logical_not(here),
             )
 
@@ -470,7 +485,20 @@
     def _():
         fr[mine] = acc[p]
 
-    sent(sends[:early])
+    sent("cz", cz.at[pl.ds(0, 2 * N - 1)])
+    sent("cy", cy.at[pl.ds(0, 2 * N - 1)])
+    gb0.sent()
+    gb1.sent()
+    ibz.sent()
+    for b in range(2):
+        sent(("grad", b), gx.at[pl.ds(0, N), b])
+        sent(("act", b), ix.at[pl.ds(0, N), b])
+        sent(("on", True, b), gx.at[pl.ds(0, N - 1), b])
+        sent(("on", False, b), ix.at[pl.ds(0, N - 1), b])
+        sent(("share", True, b), ri.at[b, pl.ds(0, N - 1)])
+        sent(("share", False, b), rg.at[b, pl.ds(0, N - 1)])
+        sent(("own", b, False), ra.at[b, pl.ds(0, N - 1)])
+        pl.when(jnp.logical_not(stays))(lambda: sent(("own", b, True), ra.at[b, 0]))
     t = jnp.zeros((rows, kg), F32)
     for dx in range(N):
         for dy in range(N):
@@ -483,7 +511,8 @@
         t += fr[k]
     out[...] = t * (1.0 / (2 * 128 * SEQS))
 
-    sent(sends[early:])
+    sent(("sums", False), fr.at[pl.ds(0, N * N - 1)])
+    pl.when(jnp.logical_not(here))(lambda: sent(("sums", True), fr.at[0]))
 
 
 def per_device(activations, gradients, expert_ids, sequence_ids, input_basis, output_basis):
@@ -519,7 +548,7 @@
             vmem((micro, N, PAIR, ka), BF16),
             vmem((N * N, rows, kg), F32),
             vmem((N * N, rows, kg), F32),
-            dma((256,)),
+            dma((32,)),
             dma((2 * N,)),
             dma((2 * N,)),
             dma((micro, 2 * N)),

time: 131 us -> 125 us (0.954)
  Pallas kernels: 130 us -> 123 us
    pallas_call x1, Pallas kernels: 130 us -> 123 us  [per_device(): pl.pallas_call(functools.partial(kernel, (toks, wa, wg, ka, kg, rows)), o...]
where the time goes in v3:
time: 125 us
  Pallas kernels  123 us (98%)
  local copies, waits for them, and re-layouts  1.35 us (1%)
    pallas_call x1, Pallas kernels, per_device(): pl.pallas_call(functools.partial(kernel, (toks, wa, wg, ka, kg, rows)), o...  123 us

profile of v3, /device:TPU:0, one launch (start us, length us, event | category | flops | bytes accessed | tf_op | source)
XLA Modules:
  0.0 124.6 jit_solution(14296461318286520734)
XLA Ops:
  0.0 123.3 %eigen.1 = f32[24,256]{1,0:T(8,128)} custom-call(s32[2,1,96]{2,1,0:T(1,128)} %bitcast.3, s32[2,1,96]{2,1,0:T(1,128)} %refs_1_.1, bf16[2,1,96,6144]{3,2,1,0:T(8,128)(2,1)} %refs_2_.1, bf16[2,1,96,16384]{3,2,1,0:T(8,128)(2,1)} %refs_3_.1, bf16[1,384,384]{2,1,0:T(8,128)(2,1)} %refs_4_.1, bf16[1,1024,256]{2,1,0:T(8,128)(2,1)} %refs_5_.1), custom_call_target="tpu_custom_call" | custom-call | tf_op jit(solution)/shard_map/eigen/pallas_call | solution.py:527
  123.3 1.3 %copy.8 = f32[1,24,256]{2,1,0:T(8,128)} copy(f32[1,24,256]{2,1,0:T(8,128)} %bitcast.2) | data formatting | bytes 49152

commit v4 on v3

--- a/solution.py
+++ b/solution.py
@@ -11,6 +11,7 @@
 SEQS = 4
 N = 4
 CAP = 18
+USED = 40
 PAIR = 48
 NEAR = (0, 1, 3, 2)
 TAG = 1024
@@ -323,8 +324,8 @@
             owner = (k + x) % N
             for i in range(lo, hi):
                 send(
-                    src.at[b, k, i],
-                    dst.at[b, me, up(me, NEAR[i])],
+                    src.at[b, k, i, pl.ds(0, USED)],
+                    dst.at[b, me, up(me, NEAR[i]), pl.ds(0, USED)],
                     sem.at[b, me],
                     along(owner),
                     ("share", src is io, b),
@@ -345,23 +346,23 @@
     for d in (1, 3):
         hand_on(gx, s_gx, 0, up(z, d))
     for d in NEAR:
+        ibz.relay(d)
+    for d in NEAR:
         pack_act(0, d)
     arrived(ib.at[x, z], s_loc.at[5])
+    for d in NEAR:
+        gb0.relay(d)
     for d in close:
         pack_grad(0, d)
-    for d in NEAR:
-        ibz.relay(d)
     rotate_in(0, close)
     share_in(0, close)
     hand_on(gx, s_gx, 0, up(z, 2))
     for d in NEAR:
-        gb0.relay(d)
+        gb1.relay(d)
     pack_grad(0, 2)
     local_rows(1)
     for d in (1, 3, 2):
         hand_on(ix, s_ix, 1, up(y, d))
-    for d in NEAR:
-        gb1.relay(d)
     for d in NEAR:
         pack_act(1, d)
     rotate_in(1, close)
@@ -397,26 +398,26 @@
     def owned(src, dst, sem, me, b, store):
         for d in (1, 3, 2):
             k = up(me, d)
-            arrived(dst.at[b, k], sem.at[b, k])
+            arrived(dst.at[b, k, :, pl.ds(0, USED)], sem.at[b, k])
         for i, d in enumerate(NEAR):
             q = up(me, d)
-            t = src[b, up(me, N - x), i].astype(F32)
+            t = src[b, up(me, N - x), i, :USED].astype(F32)
             for j in (1, 3, 2):
-                t += dst[b, up(me, j), q].astype(F32)
+                t += dst[b, up(me, j), q, :USED].astype(F32)
             store(q, t.astype(BF16))
 
     stays = y == z
 
     def owners(b):
         def store(q, value):
-            rs[b, q] = value
+            rs[b, q, :USED] = value
 
         owned(io, ri, s_ri, y, b, store)
         for d in (1, 3, 2, 0):
             k = up(y, d)
             send(
-                rs.at[b, k],
-                ra.at[b, z],
+                rs.at[b, k, pl.ds(0, USED)],
+                ra.at[b, z, pl.ds(0, USED)],
                 s_ra.at[b, z],
                 dev(x, k, y, c),
                 ("own", b, d == 0),
@@ -425,31 +426,31 @@
 
         @pl.when(stays)
         def _():
-            ra[b, z] = rs[b, y]
+            ra[b, z, :USED] = rs[b, y, :USED]
 
     def contract(b):
         def store(q, value):
-            rg[b, z, q] = value
+            rg[b, z, q, :USED] = value
 
         owned(go, rg, s_rg, z, b, store)
         for d in range(N):
             k = up(z, d)
             if d == 0:
-                pl.when(jnp.logical_not(stays))(lambda: arrived(ra.at[b, k], s_ra.at[b, k]))
+                pl.when(jnp.logical_not(stays))(lambda: arrived(ra.at[b, k, pl.ds(0, USED)], s_ra.at[b, k]))
             else:
-                arrived(ra.at[b, k], s_ra.at[b, k])
+                arrived(ra.at[b, k, pl.ds(0, USED)], s_ra.at[b, k])
 
         def one(k, _):
             numbers = cz[2 * k, b : b + 1, : 2 * toks] + cz[2 * k + 1, b : b + 1, : 2 * toks]
             labels = (
                 cz[2 * k, 2 + b : 3 + b, : 2 * toks] + cz[2 * k + 1, 2 + b : 3 + b, : 2 * toks]
             )
-            mine = lax.broadcasted_iota(jnp.int32, (PAIR, 2 * toks), 0) + (
+            mine = lax.broadcasted_iota(jnp.int32, (USED, 2 * toks), 0) + (
                 1 + c * TAG + up(z, N - x) * PAIR
             )
             label = jnp.sum(jnp.where(numbers == mine, labels, 0), axis=1, keepdims=True)
-            left = ra[b, k].astype(F32).T.astype(BF16)
-            right = rg[b, z, k].astype(F32)
+            left = ra[b, k, :USED].astype(F32).T.astype(BF16)
+            right = rg[b, z, k, :USED].astype(F32)
             for r in range(0, ka, 96):
                 rows_of = left[r : r + 96]
                 t = jnp.zeros((96, kg), F32)
@@ -495,10 +496,10 @@
         sent(("act", b), ix.at[pl.ds(0, N), b])
         sent(("on", True, b), gx.at[pl.ds(0, N - 1), b])
         sent(("on", False, b), ix.at[pl.ds(0, N - 1), b])
-        sent(("share", True, b), ri.at[b, pl.ds(0, N - 1)])
-        sent(("share", False, b), rg.at[b, pl.ds(0, N - 1)])
-        sent(("own", b, False), ra.at[b, pl.ds(0, N - 1)])
-        pl.when(jnp.logical_not(stays))(lambda: sent(("own", b, True), ra.at[b, 0]))
+        sent(("share", True, b), ri.at[b, pl.ds(0, N - 1), :, pl.ds(0, USED)])
+        sent(("share", False, b), rg.at[b, pl.ds(0, N - 1), :, pl.ds(0, USED)])
+        sent(("own", b, False), ra.at[b, pl.ds(0, N - 1), pl.ds(0, USED)])
+        pl.when(jnp.logical_not(stays))(lambda: sent(("own", b, True), ra.at[b, 0, pl.ds(0, USED)]))
     t = jnp.zeros((rows, kg), F32)
     for dx in range(N):
         for dy in range(N):

time: 125 us -> 124 us (level)
  Pallas kernels: 123 us -> 121 us
    pallas_call x1, Pallas kernels: 123 us -> 121 us  [per_device(): pl.pallas_call(functools.partial(kernel, (toks, wa, wg, ka, kg, rows)), o...]
where the time goes in v4:
time: 124 us; the launch traced here: 123 us
  Pallas kernels  121 us (98%)
  local copies, waits for them, and re-layouts  1.35 us (1%)
    pallas_call x1, Pallas kernels, per_device(): pl.pallas_call(functools.partial(kernel, (toks, wa, wg, ka, kg, rows)), o...  121 us

profile of v4, /device:TPU:0, one launch (start us, length us, event | category | flops | bytes accessed | tf_op | source)
XLA Modules:
  0.0 122.5 jit_solution(17474050273790414977)
XLA Ops:
  0.0 121.2 %eigen.1 = f32[24,256]{1,0:T(8,128)} custom-call(s32[2,1,96]{2,1,0:T(1,128)} %bitcast.3, s32[2,1,96]{2,1,0:T(1,128)} %refs_1_.1, bf16[2,1,96,6144]{3,2,1,0:T(8,128)(2,1)} %refs_2_.1, bf16[2,1,96,16384]{3,2,1,0:T(8,128)(2,1)} %refs_3_.1, bf16[1,384,384]{2,1,0:T(8,128)(2,1)} %refs_4_.1, bf16[1,1024,256]{2,1,0:T(8,128)(2,1)} %refs_5_.1), custom_call_target="tpu_custom_call" | custom-call | tf_op jit(solution)/shard_map/eigen/pallas_call | solution.py:528
  121.2 1.3 %copy.8 = f32[1,24,256]{2,1,0:T(8,128)} copy(f32[1,24,256]{2,1,0:T(8,128)} %bitcast.2) | data formatting | bytes 49152
